TPU v7x, 32 devices: a whole 2x2x4 slice. The times are simulated.
32 devices in a mesh: segment: 2 (over core), expert: 16 (over z, y, x).
Axes of the slice: x: 2, y: 2, z: 4, core: 2. Of those that a mesh axis runs over, the one named last changes fastest.
Arguments:
- saved_input: bfloat16 [2, 2, 1024, 2048], P('segment', None, 'expert'), may hold values from -6 to 6
- out_grad: bfloat16 [2, 1024, 2048], P(None, 'expert'), may hold values from -6 to 6
- expert_ids: int32 [2, 2, 1024, 2], P('segment', None, 'expert'), may hold values from 0 to 15, all different within a row; in each aligned block of 64 rows (0 to 63, 64 to 127, ..., all dimensions but the last counted through in order) at most 16 rows name the same one
- router_weights: float32 [2, 2, 1024, 2], P('segment', None, 'expert'), may hold values from 0.1 to 0.9
- w_gate: bfloat16 [2, 16, 2048, 384], P('segment', 'expert'), may hold values from -0.125 to 0.125
- w_up: bfloat16 [2, 16, 2048, 384], P('segment', 'expert'), may hold values from -0.125 to 0.125
- w_down: bfloat16 [2, 16, 384, 2048], P('segment', 'expert'), may hold values from -0.3125 to 0.3125
- eigenbasis: bfloat16 [2, 16, 384, 384], P('segment', 'expert'), may hold values from -0.3125 to 0.3125
Outputs:
- input_grad: bfloat16 [2, 2, 1024, 2048], P('segment', None, 'expert')
- rotated_grad: bfloat16 [2, 16, 384, 2048], P('segment', 'expert')
- ekfac_scales: float32 [2, 16, 384, 2048], P('segment', 'expert')
Inputs may be any that keep to these rules, and one draw needn't show every extreme that they name: `expert_ids`: the two experts of a token differ. In each layer and micro-batch, at most 16 rows of one block of 64 tokens choose the same expert, and some block reaches 16.
All inputs are finite; a program needn't handle non-finite values.
Results may differ from a plain program's by a relative error of at most 0.0085.
Values may be sent and summed in bfloat16 or wider, within the bound.
A program may use at most 128 MiB of HBM per device.

v0:
```python
import jax
import jax.numpy as jnp
from jax import lax
from jax.sharding import PartitionSpec as P


def passed_along(block, axis, distance):
    devices = range(lax.axis_size(axis))
    route = [(i - distance, i) for i in devices if i - distance in devices]
    return lax.ppermute(block, axis, route)


def silu_parts(hidden_gate):
    sigma = jax.nn.sigmoid(hidden_gate)
    return (hidden_gate * sigma, sigma * (1.0 + hidden_gate * (1.0 - sigma)))


def project_forward(x_rows, gate_mat, up_mat):
    hidden_gate = jnp.dot(x_rows, gate_mat, preferred_element_type=jnp.float32)
    hidden_up = jnp.dot(x_rows, up_mat, preferred_element_type=jnp.float32)
    return (hidden_gate, hidden_up)


def expert_backward(hidden_gate, hidden_up, dy_rows, gate_mat, up_mat, down_mat, basis):
    act, dact = silu_parts(hidden_gate)
    activ = (act * hidden_up).astype(jnp.bfloat16)
    grad_act = lax.dot_general(
        dy_rows, down_mat, (((1,), (1,)), ((), ())), preferred_element_type=jnp.float32
    )
    grad_gate = (grad_act * hidden_up * dact).astype(jnp.bfloat16)
    grad_up = (grad_act * act).astype(jnp.bfloat16)
    dx_rows = (
        lax.dot_general(
            grad_gate, gate_mat, (((1,), (1,)), ((), ())), preferred_element_type=jnp.float32
        )
        + lax.dot_general(
            grad_up, up_mat, (((1,), (1,)), ((), ())), preferred_element_type=jnp.float32
        )
    ).astype(jnp.bfloat16)
    rotated = jnp.dot(activ, basis, preferred_element_type=jnp.float32).astype(jnp.bfloat16)
    rot_sq = (rotated.astype(jnp.float32) ** 2).astype(jnp.bfloat16)
    dy_sq = (dy_rows.astype(jnp.float32) ** 2).astype(jnp.bfloat16)
    return (dx_rows, rotated, rot_sq, dy_sq)


def dispatch_matrix(ids, expert_count, capacity):
    flat = ids.reshape(-1)
    pairs = flat.shape[0]
    onehot = (flat[:, None] == jnp.arange(expert_count, dtype=jnp.int32)[None, :]).astype(
        jnp.float32
    )
    row_pos = lax.broadcasted_iota(jnp.int32, (pairs, pairs), 0)
    col_pos = lax.broadcasted_iota(jnp.int32, (pairs, pairs), 1)
    earlier = (row_pos > col_pos).astype(jnp.float32)
    prior = jnp.dot(
        earlier, onehot, precision=lax.Precision.HIGHEST, preferred_element_type=jnp.float32
    )
    rank = jnp.sum(prior * onehot, axis=1).astype(jnp.int32)
    slots = flat * capacity + rank
    targets = jnp.arange(expert_count * capacity, dtype=jnp.int32)
    return (targets[:, None] == slots[None, :]).astype(jnp.bfloat16)


def spread_rows(matrix, token_rows):
    return jnp.dot(matrix, token_rows, preferred_element_type=jnp.float32).astype(jnp.bfloat16)


def shards(saved_input, out_grad, expert_ids, router_weights, w_gate, w_up, w_down, eigenbasis):
    segment_count = lax.axis_size("segment")
    expert_count = lax.axis_size("expert")
    segment_here = lax.axis_index("segment")
    micro_count = saved_input.shape[1]
    tokens_dev = saved_input.shape[2]
    width = saved_input.shape[3]
    capacity = max(2, 4 * tokens_dev // expert_count)
    buffer_rows = expert_count * capacity
    gate_mat = w_gate[0, 0]
    up_mat = w_up[0, 0]
    down_mat = w_down[0, 0]
    basis = eigenbasis[0, 0]
    hidden_width = gate_mat.shape[1]
    matrices = jnp.stack(
        [
            dispatch_matrix(expert_ids[0, micro], expert_count, capacity)
            for micro in range(micro_count)
        ]
    )
    x_send = jnp.stack(
        [
            spread_rows(matrices[micro], jnp.repeat(saved_input[0, micro], 2, axis=0))
            for micro in range(micro_count)
        ]
    )
    x_recv = lax.all_to_all(
        x_send.reshape(micro_count, expert_count, capacity, width),
        "expert",
        split_axis=1,
        concat_axis=1,
        tiled=True,
    )
    gate_all, up_all = project_forward(
        x_recv.reshape(micro_count * buffer_rows, width), gate_mat, up_mat
    )
    gate_all = gate_all.reshape(micro_count, buffer_rows, hidden_width)
    up_all = up_all.reshape(micro_count, buffer_rows, hidden_width)
    rotated_list = []
    dy_list = []
    rot_sq_list = []
    dy_sq_list = []
    grads_out = jnp.zeros((micro_count, tokens_dev, width), jnp.bfloat16)
    received = jnp.zeros((tokens_dev, width), jnp.bfloat16)
    zero_rows = jnp.zeros((tokens_dev, width), jnp.bfloat16)
    total_ticks = micro_count + segment_count - 1
    for tick_index in range(total_ticks):
        micro_now = tick_index - (segment_count - 1 - segment_here)
        valid = jnp.logical_and(micro_now >= 0, micro_now < micro_count)
        index = jnp.clip(micro_now, 0, micro_count - 1)
        last_grad = lax.dynamic_index_in_dim(out_grad, index, 0, keepdims=False)
        upstream = jnp.where(segment_here == segment_count - 1, last_grad, received)
        upstream = jnp.where(valid, upstream, zero_rows)
        matrix = lax.dynamic_index_in_dim(matrices, index, 0, keepdims=False)
        weights_now = lax.dynamic_index_in_dim(router_weights[0], index, 0, keepdims=False)
        dy_tok = (
            weights_now.reshape(-1, 1) * jnp.repeat(upstream.astype(jnp.float32), 2, axis=0)
        ).astype(jnp.bfloat16)
        dy_send = spread_rows(matrix, dy_tok).reshape(expert_count, capacity, width)
        dy_rows = lax.all_to_all(
            dy_send, "expert", split_axis=0, concat_axis=0, tiled=True
        ).reshape(buffer_rows, width)
        hidden_gate = lax.dynamic_index_in_dim(gate_all, index, 0, keepdims=False)
        hidden_up = lax.dynamic_index_in_dim(up_all, index, 0, keepdims=False)
        dx_rows, rotated, rot_sq, dy_sq = expert_backward(
            hidden_gate, hidden_up, dy_rows, gate_mat, up_mat, down_mat, basis
        )
        rotated_list.append(rotated)
        dy_list.append(dy_rows)
        rot_sq_list.append(rot_sq)
        dy_sq_list.append(dy_sq)
        back = lax.all_to_all(
            dx_rows.reshape(expert_count, capacity, width),
            "expert",
            split_axis=0,
            concat_axis=0,
            tiled=True,
        ).reshape(buffer_rows, width)
        picked = lax.dot_general(
            matrix, back, (((0,), (0,)), ((), ())), preferred_element_type=jnp.float32
        ).reshape(tokens_dev, 2, width)
        grad_in = (upstream.astype(jnp.float32) + picked[:, 0] + picked[:, 1]).astype(jnp.bfloat16)
        updated = lax.dynamic_update_index_in_dim(grads_out, grad_in, index, 0)
        grads_out = jnp.where(valid, updated, grads_out)
        if tick_index + 1 < total_ticks:
            received = passed_along(grad_in, "segment", -1)
    all_rotated = jnp.concatenate(rotated_list, axis=0)
    all_dy = jnp.concatenate(dy_list, axis=0)
    all_rot_sq = jnp.concatenate(rot_sq_list, axis=0)
    all_dy_sq = jnp.concatenate(dy_sq_list, axis=0)
    grad_sum = lax.dot_general(
        all_rotated, all_dy, (((0,), (0,)), ((), ())), preferred_element_type=jnp.float32
    )
    scale_sum = lax.dot_general(
        all_rot_sq, all_dy_sq, (((0,), (0,)), ((), ())), preferred_element_type=jnp.float32
    )
    rotated_grad = (grad_sum * (1.0 / micro_count)).astype(jnp.bfloat16)
    ekfac_scales = scale_sum * (1.0 / micro_count)
    return (grads_out[None], rotated_grad[None, None], ekfac_scales[None, None])


def solution(mesh):
    in_specs = (
        P("segment", None, "expert", None),
        P(None, "expert", None),
        P("segment", None, "expert", None),
        P("segment", None, "expert", None),
        P("segment", "expert", None, None),
        P("segment", "expert", None, None),
        P("segment", "expert", None, None),
        P("segment", "expert", None, None),
    )
    out_specs = (
        P("segment", None, "expert", None),
        P("segment", "expert", None, None),
        P("segment", "expert", None, None),
    )
    return jax.shard_map(shards, mesh=mesh, in_specs=in_specs, out_specs=out_specs, check_vma=False)
```

profile of v0, /device:TPU:28, one launch (start us, length us, event | category | flops | bytes accessed | tf_op | source)
XLA Modules:
  0.0 287.6 jit_solution(5206329980898030522)
XLA Ops:
  4.9 1.5 convolution_convert_fusion.4
  6.4 6.9 %all-to-all-start = ((bf16[16,16,2048]{2,1,0:T(8,128)(2,1)}), bf16[16,16,2048]{2,1,0:T(8,128)(2,1)}, u32[]{:S(2)}, u32[]{:S(2)}) async-start(bf16[16,16,2048]{2,1,0:T(8,128)(2,1)} %bitcast.4), calls=%async_computation | async-start | bytes 2097152 | tf_op jit(solution)/shard_map/all_to_all | solution.py:127
  15.3 1.5 pad_maximum_fusion
  16.8 20.9 %all-to-all-done = bf16[16,16,2048]{2,1,0:T(8,128)(2,1)} async-done(((bf16[16,16,2048]{2,1,0:T(8,128)(2,1)}), bf16[16,16,2048]{2,1,0:T(8,128)(2,1)}, u32[]{:S(2)}, u32[]{:S(2)}) %all-to-all-start) | async-done | bytes 1048608 | tf_op jit(solution)/shard_map/all_to_all | solution.py:127
  37.7 6.0 %all-to-all-start.1 = ((bf16[2,16,16,2048]{3,2,0,1:T(8,128)(2,1)}), bf16[2,16,16,2048]{3,2,0,1:T(8,128)(2,1)}, u32[]{:S(2)}, u32[]{:S(2)}) async-start(bf16[2,16,16,2048]{3,2,0,1:T(8,128)(2,1)} %pad_maximum_fusion), calls=%async_computation.1 | async-start | bytes 4194304 | tf_op jit(solution)/shard_map/all_to_all | solution.py:94
  43.7 1.9 fusion.39
  45.7 43.7 %all-to-all-done.1 = bf16[2,16,16,2048]{3,2,0,1:T(8,128)(2,1)} async-done(((bf16[2,16,16,2048]{3,2,0,1:T(8,128)(2,1)}), bf16[2,16,16,2048]{3,2,0,1:T(8,128)(2,1)}, u32[]{:S(2)}, u32[]{:S(2)}) %all-to-all-start.1) | async-done | bytes 2097184 | tf_op jit(solution)/shard_map/all_to_all | solution.py:94
  89.3 1.8 copy.29
  91.4 1.2 fusion.24
  92.7 1.3 fusion.22
  94.8 1.7 fusion.19
  96.6 6.2 %all-to-all-start.2 = ((bf16[16,16,2048]{2,1,0:T(8,128)(2,1)}), bf16[16,16,2048]{2,1,0:T(8,128)(2,1)}, u32[]{:S(2)}, u32[]{:S(2)}) async-start(bf16[16,16,2048]{2,1,0:T(8,128)(2,1)} %bitcast.332), calls=%async_computation.2 | async-start | bytes 2097152 | tf_op jit(solution)/shard_map/all_to_all | solution.py:139
  102.8 23.4 %all-to-all-done.2 = bf16[16,16,2048]{2,1,0:T(8,128)(2,1)} async-done(((bf16[16,16,2048]{2,1,0:T(8,128)(2,1)}), bf16[16,16,2048]{2,1,0:T(8,128)(2,1)}, u32[]{:S(2)}, u32[]{:S(2)}) %all-to-all-start.2) | async-done | bytes 1048608 | tf_op jit(solution)/shard_map/all_to_all | solution.py:139
  126.2 1.6 fusion.128
  129.5 1.3 collective-permute-start
  130.9 2.2 collective-permute-done
  133.2 1.0 fusion.102
  135.0 1.2 multiply_convert_fusion.5
  136.2 2.0 convert_element_type.225
  138.2 1.5 convolution_convert_fusion.1
  139.7 30.6 %all_to_all.35 = bf16[16,16,2048]{2,1,0:T(8,128)(2,1)S(1)} all-to-all(bf16[16,16,2048]{2,1,0:T(8,128)(2,1)S(1)} %bitcast.329), channel_id=1, replica_groups=mesh['segment'=2,'expert'=16] {'expert'}, dimensions={0} | all-to-all | bytes 2097152 | tf_op jit(solution)/shard_map/all_to_all | solution.py:127
  170.4 1.0 copy-done.5
  173.5 1.7 fusion.20
  175.3 6.5 %all-to-all-start.4 = ((bf16[16,16,2048]{2,1,0:T(8,128)(2,1)}), bf16[16,16,2048]{2,1,0:T(8,128)(2,1)}, u32[]{:S(2)}, u32[]{:S(2)}) async-start(bf16[16,16,2048]{2,1,0:T(8,128)(2,1)} %bitcast.331), calls=%async_computation.4 | async-start | bytes 2097152 | tf_op jit(solution)/shard_map/all_to_all | solution.py:139
  182.7 2.1 fusion.97
  184.7 20.2 %all-to-all-done.4 = bf16[16,16,2048]{2,1,0:T(8,128)(2,1)} async-done(((bf16[16,16,2048]{2,1,0:T(8,128)(2,1)}), bf16[16,16,2048]{2,1,0:T(8,128)(2,1)}, u32[]{:S(2)}, u32[]{:S(2)}) %all-to-all-start.4) | async-done | bytes 1048608 | tf_op jit(solution)/shard_map/all_to_all | solution.py:139
  204.9 1.6 fusion.126
  206.5 1.8 fusion.100
  208.3 1.4 collective-permute-start.1
  209.8 2.2 collective-permute-done.1
  212.0 1.1 fusion.99
  213.9 1.2 multiply_convert_fusion.4
  215.1 2.0 convert_element_type.233
  217.1 2.5 convolution_convert_fusion
  219.6 6.0 %all-to-all-start.5 = ((bf16[16,16,2048]{2,1,0:T(8,128)(2,1)}), bf16[16,16,2048]{2,1,0:T(8,128)(2,1)}, u32[]{:S(2)}, u32[]{:S(2)}) async-start(bf16[16,16,2048]{2,1,0:T(8,128)(2,1)} %bitcast.328), calls=%async_computation.5 | async-start | bytes 2097152 | tf_op jit(solution)/shard_map/all_to_all | solution.py:127
  225.7 2.5 multiply_convert_fusion.3
  228.2 2.0 multiply_convert_fusion.7
  230.2 20.0 %all-to-all-done.5 = bf16[16,16,2048]{2,1,0:T(8,128)(2,1)} async-done(((bf16[16,16,2048]{2,1,0:T(8,128)(2,1)}), bf16[16,16,2048]{2,1,0:T(8,128)(2,1)}, u32[]{:S(2)}, u32[]{:S(2)}) %all-to-all-start.5) | async-done | bytes 1048608 | tf_op jit(solution)/shard_map/all_to_all | solution.py:127
  250.2 2.1 fusion.35
  253.7 1.7 fusion.21
  255.4 6.2 %all-to-all-start.6 = ((bf16[16,16,2048]{2,1,0:T(8,128)(2,1)}), bf16[16,16,2048]{2,1,0:T(8,128)(2,1)S(1)}, u32[]{:S(2)}, u32[]{:S(2)}) async-start(bf16[16,16,2048]{2,1,0:T(8,128)(2,1)} %bitcast.330), calls=%async_computation.6 | async-start | bytes 2097152 | tf_op jit(solution)/shard_map/all_to_all | solution.py:139
  261.7 1.5 multiply_convert_fusion.8
  263.8 1.9 copy.43
  265.7 4.1 %fusion.16 = bf16[1,1,384,2048]{3,2,1,0:T(8,128)(2,1)} fusion(bf16[256,2048]{1,0:T(8,128)(2,1)} %bitcast.47, bf16[256,2048]{1,0:T(8,128)(2,1)S(1)} %bitcast.326, bf16[256,2048]{1,0:T(8,128)(2,1)} %bitcast.5, bf16[256,384]{1,0:T(8,128)(2,1)S(1)} %copy-done.34, bf16[256,384]{1,0:T(8,128)(2,1)S(1)} %get-tuple-element.18, ...), kind=kOutput, calls=%fused_computation.17 | convolution fusion | flops 1220739072 | bytes 5308416 | tf_op jit(solution)/shard_map/dot_general | solution.py:158
  269.8 1.6 multiply_convert_fusion.1
  271.4 3.1 %multiply_bitcast_fusion = f32[1,1,384,2048]{3,2,1,0:T(8,128)} fusion(bf16[256,2048]{1,0:T(8,128)(2,1)S(1)} %multiply_convert_fusion.1, bf16[256,2048]{1,0:T(8,128)(2,1)S(1)} %multiply_convert_fusion.2, bf16[256,2048]{1,0:T(8,128)(2,1)S(1)} %copy-done.23, bf16[256,384]{1,0:T(8,128)(2,1)S(1)} %copy-done.33, bf16[256,384]{1,0:T(8,128)(2,1)S(1)} %get-tuple-element.17, ...), kind=kOutput, calls=%fused_computation.12 | convolution fusion | flops 1219952640 | bytes 6881280 | tf_op jit(solution)/shard_map/dot_general | solution.py:161
  274.5 10.2 %all-to-all-done.6 = bf16[16,16,2048]{2,1,0:T(8,128)(2,1)S(1)} async-done(((bf16[16,16,2048]{2,1,0:T(8,128)(2,1)}), bf16[16,16,2048]{2,1,0:T(8,128)(2,1)S(1)}, u32[]{:S(2)}, u32[]{:S(2)}) %all-to-all-start.6) | async-done | bytes 1048608 | tf_op jit(solution)/shard_map/all_to_all | solution.py:139
  285.8 1.0 fusion.95
  (106 shorter events, 17.7 us)
Async XLA Ops:
  0.6 92.0 %copy-start = (bf16[1,1,2048,384]{3,2,1,0:T(8,128)(2,1)S(1)}, bf16[1,1,2048,384]{3,2,1,0:T(8,128)(2,1)}, u32[]{:S(2)}) copy-start(bf16[1,1,2048,384]{3,2,1,0:T(8,128)(2,1)} %param.12) | copy-start | bytes 4718596
  0.6 2.6 copy-start.31
  3.2 10.1 %copy-start.24 = (bf16[1,2,64,2048]{3,2,1,0:T(8,128)(2,1)S(1)}, bf16[1,2,64,2048]{3,2,1,0:T(8,128)(2,1)}, u32[]{:S(2)}) copy-start(bf16[1,2,64,2048]{3,2,1,0:T(8,128)(2,1)} %param.8) | copy-start | bytes 1572868
  4.9 1.5 copy-start.29
  6.4 31.3 %all-to-all-start = ((bf16[16,16,2048]{2,1,0:T(8,128)(2,1)}), bf16[16,16,2048]{2,1,0:T(8,128)(2,1)}, u32[]{:S(2)}, u32[]{:S(2)}) async-start(bf16[16,16,2048]{2,1,0:T(8,128)(2,1)} %bitcast.4), calls=%async_computation | async-start | bytes 2097152 | tf_op jit(solution)/shard_map/all_to_all | solution.py:127
  16.8 26.9 %copy-start.1 = (bf16[1,1,384,2048]{3,2,1,0:T(8,128)(2,1)S(1)}, bf16[1,1,384,2048]{3,2,1,0:T(8,128)(2,1)}, u32[]{:S(2)}) copy-start(bf16[1,1,384,2048]{3,2,1,0:T(8,128)(2,1)} %param.14) | copy-start | bytes 4718596
  37.7 51.6 %all-to-all-start.1 = ((bf16[2,16,16,2048]{3,2,0,1:T(8,128)(2,1)}), bf16[2,16,16,2048]{3,2,0,1:T(8,128)(2,1)}, u32[]{:S(2)}, u32[]{:S(2)}) async-start(bf16[2,16,16,2048]{3,2,0,1:T(8,128)(2,1)} %pad_maximum_fusion), calls=%async_computation.1 | async-start | bytes 4194304 | tf_op jit(solution)/shard_map/all_to_all | solution.py:94
  89.3 2.0 copy-start.2
  92.6 1.3 copy-start.18
  93.9 0.9 copy-start.8
  96.6 6.2 %copy-start.30 = (pred[1,256,128]{1,2,0:T(32,128)(4,1)S(1)}, pred[1,256,128]{1,2,0:T(32,128)(4,1)}, u32[]{:S(2)}) copy-start(pred[1,256,128]{1,2,0:T(32,128)(4,1)} %copy-done.29) | copy-start | bytes 98308
  96.6 29.6 %all-to-all-start.2 = ((bf16[16,16,2048]{2,1,0:T(8,128)(2,1)}), bf16[16,16,2048]{2,1,0:T(8,128)(2,1)}, u32[]{:S(2)}, u32[]{:S(2)}) async-start(bf16[16,16,2048]{2,1,0:T(8,128)(2,1)} %bitcast.332), calls=%async_computation.2 | async-start | bytes 2097152 | tf_op jit(solution)/shard_map/all_to_all | solution.py:139
  126.2 2.6 copy-start.17
  127.8 1.0 copy-start.7
  128.7 9.5 %copy-start.28 = (pred[1,256,128]{1,2,0:T(32,128)(4,1)S(1)}, pred[1,256,128]{1,2,0:T(32,128)(4,1)}, u32[]{:S(2)}) copy-start(pred[1,256,128]{1,2,0:T(32,128)(4,1)} %get-tuple-element.9) | copy-start | bytes 98308
  129.5 3.6 %collective-permute-start = (bf16[64,2048]{1,0:T(8,128)(2,1)}, bf16[64,2048]{1,0:T(8,128)(2,1)S(1)}, u32[]{:S(2)}, u32[]{:S(2)}) collective-permute-start(bf16[64,2048]{1,0:T(8,128)(2,1)} %fusion.61), channel_id=1, source_target_pairs={{16,0},{17,1},{18,2},{19,3},{20,4},{21,5},{22,6},{23,7},{24,8},{25... | collective-permute-start | bytes 786440 | tf_op jit(solution)/shard_map/ppermute | solution.py:10
  134.2 0.8 copy-start.15
  139.7 32.4 %copy-start.9 = (f32[2,256,384]{2,1,0:T(8,128)S(1)}, f32[2,256,384]{2,1,0:T(8,128)}, u32[]{:S(2)}) copy-start(f32[2,256,384]{2,1,0:T(8,128)} %copy-done.8) | copy-start | bytes 2359300
  139.7 32.4 %copy-start.19 = (f32[2,256,384]{2,1,0:T(8,128)S(1)}, f32[2,256,384]{2,1,0:T(8,128)}, u32[]{:S(2)}) copy-start(f32[2,256,384]{2,1,0:T(8,128)} %copy-done.18) | copy-start | bytes 2359300
  170.4 1.0 copy-start.5
  172.1 1.4 copy-start.3
  175.3 29.7 %all-to-all-start.4 = ((bf16[16,16,2048]{2,1,0:T(8,128)(2,1)}), bf16[16,16,2048]{2,1,0:T(8,128)(2,1)}, u32[]{:S(2)}, u32[]{:S(2)}) async-start(bf16[16,16,2048]{2,1,0:T(8,128)(2,1)} %bitcast.331), calls=%async_computation.4 | async-start | bytes 2097152 | tf_op jit(solution)/shard_map/all_to_all | solution.py:139
  204.9 1.6 copy-start.16
  208.3 8.8 %copy-start.27 = (pred[1,256,128]{1,2,0:T(32,128)(4,1)S(1)}, pred[1,256,128]{1,2,0:T(32,128)(4,1)}, u32[]{:S(2)}) copy-start(pred[1,256,128]{1,2,0:T(32,128)(4,1)} %get-tuple-element.7) | copy-start | bytes 98308
  208.3 3.7 %collective-permute-start.1 = (bf16[64,2048]{1,0:T(8,128)(2,1)S(1)}, bf16[64,2048]{1,0:T(8,128)(2,1)}, u32[]{:S(2)}, u32[]{:S(2)}) collective-permute-start(bf16[64,2048]{1,0:T(8,128)(2,1)S(1)} %get-tuple-element.4), channel_id=1, source_target_pairs={{16,0},{17,1},{18,2},{19,3},{20,4},{21,5},{22,6},{23,7},{24,8},{25... | collective-permute-start | bytes 786440 | tf_op jit(solution)/shard_map/ppermute | solution.py:10
  213.1 0.8 copy-start.13
  219.6 30.6 %all-to-all-start.5 = ((bf16[16,16,2048]{2,1,0:T(8,128)(2,1)}), bf16[16,16,2048]{2,1,0:T(8,128)(2,1)}, u32[]{:S(2)}, u32[]{:S(2)}) async-start(bf16[16,16,2048]{2,1,0:T(8,128)(2,1)} %bitcast.328), calls=%async_computation.5 | async-start | bytes 2097152 | tf_op jit(solution)/shard_map/all_to_all | solution.py:127
  225.7 2.5 copy-start.10
  225.7 2.5 copy-start.20
  250.2 2.1 copy-start.11
  250.2 2.1 copy-start.21
  252.3 1.4 copy-start.4
  255.4 6.2 %copy-start.12 = (f32[2,256,384]{2,1,0:T(8,128)S(1)}, f32[2,256,384]{2,1,0:T(8,128)}, u32[]{:S(2)}) copy-start(f32[2,256,384]{2,1,0:T(8,128)} %copy-done.8) | copy-start | bytes 2359300
  255.4 29.3 %all-to-all-start.6 = ((bf16[16,16,2048]{2,1,0:T(8,128)(2,1)}), bf16[16,16,2048]{2,1,0:T(8,128)(2,1)S(1)}, u32[]{:S(2)}, u32[]{:S(2)}) async-start(bf16[16,16,2048]{2,1,0:T(8,128)(2,1)} %bitcast.330), calls=%async_computation.6 | async-start | bytes 2097152 | tf_op jit(solution)/shard_map/all_to_all | solution.py:139
  261.6 1.6 copy-start.22
  261.6 1.6 copy-start.32
  261.7 1.9 copy-start.6
  263.5 2.2 copy-start.34
  269.8 1.6 copy-start.23
  269.8 1.6 copy-start.33
  274.5 10.5 %copy-start.14 = (f32[64,2048]{1,0:T(8,128)S(1)}, f32[64,2048]{1,0:T(8,128)}, u32[]{:S(2)}) copy-start(f32[64,2048]{1,0:T(8,128)} %copy-done.13) | copy-start | bytes 1572868
  284.7 1.0 copy-start.25
  286.8 0.8 copy-start.26
where the time goes:
time: 291 us; the launch traced here: 288 us
  waiting for transfers between devices  143 us (49%)
  starting transfers between devices  40.6 us (14%)
  matrix products  36 us (12%)
  blocking collectives  30.6 us (11%)
  other arithmetic  18.4 us (6%)
  local copies, waits for them, and re-layouts  18.2 us (6%)
    all_to_all x3, waiting for transfers between devices, shards(): lax.all_to_all(dx_rows.reshape(expert_count, capacity, width), 'expert',...  53.7 us
    all_to_all x1, waiting for transfers between devices, shards(): lax.all_to_all(x_send.reshape(micro_count, expert_count, capacity, width)...  43.7 us
    all_to_all x2, waiting for transfers between devices, shards(): lax.all_to_all(dy_send, 'expert', split_axis=0, concat_axis=0, tiled=True)  40.9 us
    all_to_all x1, blocking collectives, shards(): lax.all_to_all(dy_send, 'expert', split_axis=0, concat_axis=0, tiled=True)  30.6 us
    all_to_all x3, starting transfers between devices, shards(): lax.all_to_all(dx_rows.reshape(expert_count, capacity, width), 'expert',...  18.9 us
    all_to_all x2, starting transfers between devices, shards(): lax.all_to_all(dy_send, 'expert', split_axis=0, concat_axis=0, tiled=True)  13 us
    unnamed x71, local copies, waits for them, and re-layouts  8.5 us
    dot_general x5, matrix products, spread_rows(): jnp.dot(matrix, token_rows, preferred_element_type=jnp.float32)  6.31 us
  transfers between devices with their start and end apart: 8, of which 8 were waited for; matrix products, arithmetic and copies ran while one was open for 9% of the time, Pallas kernels for 0%

commit v1 on v0

--- a/solution.py
+++ b/solution.py
@@ -1,6 +1,10 @@
+import functools
+
 import jax
 import jax.numpy as jnp
 from jax import lax
+from jax.experimental import pallas as pl
+from jax.experimental.pallas import tpu as pltpu
 from jax.sharding import PartitionSpec as P
 
 
@@ -166,6 +170,376 @@
     return (grads_out[None], rotated_grad[None, None], ekfac_scales[None, None])
 
 
+def dot_f32(a, b, dims):
+    return lax.dot_general(a, b, (dims, ((), ())), preferred_element_type=jnp.float32)
+
+
+def relay_kernel(
+    cap,
+    x_ref,
+    og_ref,
+    ids_ref,
+    rw_ref,
+    gate_hbm,
+    up_hbm,
+    down_hbm,
+    basis_hbm,
+    gin_out,
+    rot_out,
+    scale_out,
+    gate,
+    up,
+    down,
+    basis,
+    x_send,
+    x_recv,
+    dy_send,
+    dy_recv,
+    dx_send,
+    dx_recv,
+    g_recv,
+    gin,
+    hid_g,
+    hid_u,
+    rot_t,
+    rsq_t,
+    spread_x,
+    spread_dy,
+    combine,
+    rot_v,
+    scale_v,
+    w_sem,
+    send_sem,
+    recv_sem,
+    self_sem,
+    relay_send,
+    relay_recv,
+    out_sem,
+):
+    bf16 = jnp.bfloat16
+    f32 = jnp.float32
+    n = lax.axis_size("expert")
+    segs = lax.axis_size("segment")
+    me = lax.axis_index("expert")
+    seg = lax.axis_index("segment")
+    micros, tokens, width = x_ref.shape
+    rows = n * cap
+    is_last = seg == segs - 1
+    is_first = seg == 0
+    X, DY, DX = 0, 1, 2
+
+    weights = [
+        pltpu.make_async_copy(src, dst, w_sem.at[i])
+        for i, (src, dst) in enumerate(
+            ((gate_hbm, gate), (up_hbm, up), (down_hbm, down), (basis_hbm, basis))
+        )
+    ]
+    for w in weights:
+        w.start()
+
+    barrier = pltpu.get_barrier_semaphore()
+
+    def greet(d, carry):
+        pl.semaphore_signal(barrier, inc=1, device_id={"expert": lax.rem(me + d, n)})
+        return carry
+
+    lax.fori_loop(1, n, greet, 0)
+
+    @pl.when(seg > 0)
+    def _():
+        pl.semaphore_signal(barrier, inc=1, device_id={"segment": seg - 1})
+
+    @pl.when(seg < segs - 1)
+    def _():
+        pl.semaphore_signal(barrier, inc=1, device_id={"segment": seg + 1})
+
+    row_t = lax.broadcasted_iota(jnp.int32, (tokens, tokens), 0)
+    col_t = lax.broadcasted_iota(jnp.int32, (tokens, tokens), 1)
+    earlier = (row_t > col_t).astype(bf16)
+    lanes = lax.broadcasted_iota(jnp.int32, (tokens, n), 1)
+    slots_iota = lax.broadcasted_iota(jnp.int32, (tokens, rows), 1)
+    for m in range(micros):
+        ids0 = ids_ref[m, :, 0:1]
+        ids1 = ids_ref[m, :, 1:2]
+        hot0 = (lanes == ids0).astype(f32)
+        hot1 = (lanes == ids1).astype(f32)
+        prior = dot_f32(earlier, (hot0 + hot1).astype(bf16), ((1,), (0,)))
+        rank0 = jnp.sum(prior * hot0, axis=1, keepdims=True).astype(jnp.int32)
+        rank1 = jnp.sum(prior * hot1, axis=1, keepdims=True).astype(jnp.int32)
+        pick0 = (slots_iota == ids0 * cap + rank0).astype(f32)
+        pick1 = (slots_iota == ids1 * cap + rank1).astype(f32)
+        both = pick0 + pick1
+        combine[m] = both.astype(bf16)
+        spread_x[m] = jnp.transpose(both).astype(bf16)
+        spread_dy[m] = jnp.transpose(jnp.concatenate([pick0, pick1], axis=0)).astype(bf16)
+
+    def spread(m, matrix, values, dst):
+        step = min(512, width)
+        for c in range(width // step):
+            cols = slice(c * step, (c + 1) * step)
+            dst[m, :, cols] = dot_f32(matrix, values(cols), ((1,), (0,))).astype(bf16)
+
+    def block(i):
+        return pl.ds(pl.multiple_of(i * cap, cap), cap)
+
+    def push(kind, m, src, dst):
+        pltpu.make_async_copy(
+            src.at[m, block(me)], dst.at[m, block(me)], self_sem.at[kind, m]
+        ).start()
+
+        def one(d, carry):
+            peer = lax.rem(me + d, n)
+            pltpu.make_async_remote_copy(
+                src_ref=src.at[m, block(peer)],
+                dst_ref=dst.at[m, block(me)],
+                send_sem=send_sem.at[kind, m],
+                recv_sem=recv_sem.at[kind, m],
+                device_id={"expert": peer},
+            ).start()
+            return carry
+
+        lax.fori_loop(1, n, one, 0)
+
+    def whole(kind, m, src, dst):
+        part = pl.ds(0, (n - 1) * cap)
+        return pltpu.make_async_remote_copy(
+            src_ref=src.at[m, part],
+            dst_ref=dst.at[m, part],
+            send_sem=send_sem.at[kind, m],
+            recv_sem=recv_sem.at[kind, m],
+            device_id={"expert": lax.rem(me + 1, n)},
+        )
+
+    def arrive(kind, m, src, dst):
+        pltpu.make_async_copy(
+            src.at[m, block(me)], dst.at[m, block(me)], self_sem.at[kind, m]
+        ).wait()
+        whole(kind, m, src, dst).wait_recv()
+
+    def send_x(m):
+        spread(m, spread_x[m], lambda cols: x_ref[m, :, cols], x_send)
+        push(X, m, x_send, x_recv)
+
+    def send_dy(m, g_ref):
+        w0 = rw_ref[m, :, 0:1]
+        w1 = rw_ref[m, :, 1:2]
+
+        def values(cols):
+            g = g_ref[m, :, cols].astype(f32)
+            return jnp.concatenate([(w0 * g).astype(bf16), (w1 * g).astype(bf16)], axis=0)
+
+        spread(m, spread_dy[m], values, dy_send)
+        push(DY, m, dy_send, dy_recv)
+
+    def forward(m):
+        arrive(X, m, x_send, x_recv)
+        x = x_recv[m]
+        hid_g[m] = dot_f32(x, gate[...], ((1,), (0,)))
+        hid_u[m] = dot_f32(x, up[...], ((1,), (0,)))
+
+    def backward(m):
+        arrive(DY, m, dy_send, dy_recv)
+        grad_act = dot_f32(dy_recv[m], down[...], ((1,), (1,)))
+        hg = hid_g[m]
+        hu = hid_u[m]
+        act, dact = silu_parts(hg)
+        grad_gate = (grad_act * hu * dact).astype(bf16)
+        grad_up = (grad_act * act).astype(bf16)
+        step = min(512, width)
+        for c in range(width // step):
+            cols = slice(c * step, (c + 1) * step)
+            dx_send[m, :, cols] = (
+                dot_f32(grad_gate, gate[cols, :], ((1,), (1,)))
+                + dot_f32(grad_up, up[cols, :], ((1,), (1,)))
+            ).astype(bf16)
+        push(DX, m, dx_send, dx_recv)
+
+    def rotate(m):
+        act, _ = silu_parts(hid_g[m])
+        activ = (act * hid_u[m]).astype(bf16)
+        rotated = dot_f32(activ, basis[...], ((1,), (0,))).astype(bf16).astype(f32)
+        turned = jnp.transpose(rotated)
+        rot_t[m] = turned.astype(bf16)
+        rsq_t[m] = (turned * turned).astype(bf16)
+
+    def relay(m):
+        return pltpu.make_async_remote_copy(
+            src_ref=gin.at[m],
+            dst_ref=g_recv.at[m],
+            send_sem=relay_send.at[m],
+            recv_sem=relay_recv.at[m],
+            device_id={"segment": lax.rem(seg + segs - 1, segs)},
+        )
+
+    def gather_back(m, g_ref):
+        arrive(DX, m, dx_send, dx_recv)
+        step = min(512, width)
+        for c in range(width // step):
+            cols = slice(c * step, (c + 1) * step)
+            picked = dot_f32(combine[m], dx_recv[m, :, cols], ((1,), (0,)))
+            gin[m, :, cols] = (g_ref[m, :, cols].astype(f32) + picked).astype(bf16)
+
+        @pl.when(seg > 0)
+        def _():
+            relay(m).start()
+
+        pltpu.make_async_copy(gin.at[m], gin_out.at[m], out_sem.at[2 + m]).start()
+
+    def statistics():
+        step = min(256, width)
+
+        def one(c, carry):
+            cols = pl.ds(pl.multiple_of(c * step, step), step)
+            grad = jnp.zeros((rot_v.shape[0], step), f32)
+            scale = jnp.zeros((rot_v.shape[0], step), f32)
+            for m in range(micros):
+                dy = dy_recv[m, :, cols]
+                wide = dy.astype(f32)
+                grad = grad + dot_f32(rot_t[m], dy, ((1,), (0,)))
+                scale = scale + dot_f32(rsq_t[m], (wide * wide).astype(bf16), ((1,), (0,)))
+            rot_v[:, cols] = (grad * (1.0 / micros)).astype(bf16)
+            scale_v[:, cols] = scale * (1.0 / micros)
+            return carry
+
+        lax.fori_loop(0, width // step, one, 0)
+        pltpu.make_async_copy(rot_v, rot_out, out_sem.at[0]).start()
+        pltpu.make_async_copy(scale_v, scale_out, out_sem.at[1]).start()
+
+    def per_micro(fn):
+        def one(m, carry):
+            fn(m)
+            return carry
+
+        lax.fori_loop(0, micros, one, 0)
+
+    neighbours = jnp.minimum(seg, 1) + jnp.minimum(segs - 1 - seg, 1)
+    pl.semaphore_wait(barrier, n - 1 + neighbours)
+
+    @pl.when(is_last)
+    def _():
+        def first(m):
+            send_dy(m, og_ref)
+            send_x(m)
+
+        per_micro(first)
+        for w in weights:
+            w.wait()
+
+        def second(m):
+            forward(m)
+            backward(m)
+
+        per_micro(second)
+        per_micro(rotate)
+        per_micro(lambda m: gather_back(m, og_ref))
+        statistics()
+
+    @pl.when(jnp.logical_not(is_last))
+    def _():
+        per_micro(send_x)
+        for w in weights:
+            w.wait()
+        per_micro(forward)
+        per_micro(rotate)
+
+        def third(m):
+            relay(m).wait_recv()
+            send_dy(m, g_recv)
+
+        per_micro(third)
+        per_micro(backward)
+        statistics()
+        per_micro(lambda m: gather_back(m, g_recv))
+
+    def drain(m):
+        whole(X, m, x_send, x_recv).wait_send()
+        whole(DY, m, dy_send, dy_recv).wait_send()
+        whole(DX, m, dx_send, dx_recv).wait_send()
+
+        @pl.when(seg > 0)
+        def _():
+            relay(m).wait_send()
+
+        pltpu.make_async_copy(gin.at[m], gin_out.at[m], out_sem.at[2 + m]).wait()
+
+    per_micro(drain)
+    pltpu.make_async_copy(rot_v, rot_out, out_sem.at[0]).wait()
+    pltpu.make_async_copy(scale_v, scale_out, out_sem.at[1]).wait()
+
+
+def fused_shards(
+    saved_input, out_grad, expert_ids, router_weights, w_gate, w_up, w_down, eigenbasis
+):
+    n = lax.axis_size("expert")
+    micros, tokens, width = saved_input.shape[1:]
+    cap = max(2, 4 * tokens // n)
+    if cap % 16:
+        return shards(
+            saved_input, out_grad, expert_ids, router_weights, w_gate, w_up, w_down, eigenbasis
+        )
+    rows = n * cap
+    hidden = w_gate.shape[3]
+    bf16 = jnp.bfloat16
+    f32 = jnp.float32
+    vmem = pl.BlockSpec(memory_space=pltpu.VMEM)
+    anywhere = pl.BlockSpec(memory_space=pl.ANY)
+    routed = pltpu.VMEM((micros, rows, width), bf16)
+    grad_in, rotated_grad, scales = pl.pallas_call(
+        functools.partial(relay_kernel, cap),
+        name="relay",
+        out_shape=(
+            jax.ShapeDtypeStruct((micros, tokens, width), bf16),
+            jax.ShapeDtypeStruct((hidden, width), bf16),
+            jax.ShapeDtypeStruct((hidden, width), f32),
+        ),
+        in_specs=[vmem] * 4 + [anywhere] * 4,
+        out_specs=(anywhere, anywhere, anywhere),
+        scratch_shapes=[
+            pltpu.VMEM((width, hidden), bf16),
+            pltpu.VMEM((width, hidden), bf16),
+            pltpu.VMEM((hidden, width), bf16),
+            pltpu.VMEM((hidden, hidden), bf16),
+            routed,
+            routed,
+            routed,
+            routed,
+            routed,
+            routed,
+            pltpu.VMEM((micros, tokens, width), bf16),
+            pltpu.VMEM((micros, tokens, width), bf16),
+            pltpu.VMEM((micros, rows, hidden), f32),
+            pltpu.VMEM((micros, rows, hidden), f32),
+            pltpu.VMEM((micros, hidden, rows), bf16),
+            pltpu.VMEM((micros, hidden, rows), bf16),
+            pltpu.VMEM((micros, rows, tokens), bf16),
+            pltpu.VMEM((micros, rows, 2 * tokens), bf16),
+            pltpu.VMEM((micros, tokens, rows), bf16),
+            pltpu.VMEM((hidden, width), bf16),
+            pltpu.VMEM((hidden, width), f32),
+            pltpu.SemaphoreType.DMA((4,)),
+            pltpu.SemaphoreType.DMA((3, micros)),
+            pltpu.SemaphoreType.DMA((3, micros)),
+            pltpu.SemaphoreType.DMA((3, micros)),
+            pltpu.SemaphoreType.DMA((micros,)),
+            pltpu.SemaphoreType.DMA((micros,)),
+            pltpu.SemaphoreType.DMA((2 + micros,)),
+        ],
+        compiler_params=pltpu.CompilerParams(
+            collective_id=0, has_side_effects=True, vmem_limit_bytes=62 << 20
+        ),
+    )(
+        saved_input[0],
+        out_grad,
+        expert_ids[0],
+        router_weights[0],
+        w_gate[0, 0],
+        w_up[0, 0],
+        w_down[0, 0],
+        eigenbasis[0, 0],
+    )
+    return (grad_in[None], rotated_grad[None, None], scales[None, None])
+
+
 def solution(mesh):
     in_specs = (
         P("segment", None, "expert", None),
@@ -182,4 +556,5 @@
         P("segment", "expert", None, None),
         P("segment", "expert", None, None),
     )
-    return jax.shard_map(shards, mesh=mesh, in_specs=in_specs, out_specs=out_specs, check_vma=False)
+    return jax.shard_map(
+        fused_shards, mesh=mesh, in_specs=in_specs, out_specs=out_specs, check_vma=False)

time: 291 us -> 160 us (0.55); the launches traced: 288 us -> 160 us
  Pallas kernels: 0 us -> 150 us
  waiting for transfers between devices: 143 us -> 0 us
  starting transfers between devices: 40.6 us -> 0 us
  matrix products: 36 us -> 0 us
  blocking collectives: 30.6 us -> 0 us
  other arithmetic: 18.4 us -> 0 us
  local copies, waits for them, and re-layouts: 18.2 us -> 9.26 us
    pallas_call x0 -> x1, Pallas kernels: none -> 150 us  [fused_shards(): pl.pallas_call(functools.partial(relay_kernel, cap), name='relay', out_sh...]
    all_to_all x6 -> x0, waiting for transfers between devices: 138 us -> none  [the longest x3 53.7 us: shards(): lax.all_to_all(dx_rows.reshape(expert_count, capacity, width), 'expert',...]
    all_to_all x6 -> x0, starting transfers between devices: 37.9 us -> none  [the longest x3 18.9 us: shards(): lax.all_to_all(dx_rows.reshape(expert_count, capacity, width), 'expert',...]
    dot_general x26 -> x0, matrix products: 36 us -> none  [the longest x5 6.31 us: spread_rows(): jnp.dot(matrix, token_rows, preferred_element_type=jnp.float32)]
    all_to_all x1 -> x0, blocking collectives: 30.6 us -> none  [shards(): lax.all_to_all(dy_send, 'expert', split_axis=0, concat_axis=0, tiled=True)]
    convert_element_type x10 -> x0, other arithmetic: 11.1 us -> none  [the longest x3 4.38 us: expert_backward(): dy_sq = (dy_rows.astype(jnp.float32) ** 2).astype(jnp.bfloat16)]
    select_n x3 -> x0, other arithmetic: 4.91 us -> none  [shards(): grads_out = jnp.where(valid, updated, grads_out)]
    ppermute x2 -> x0, waiting for transfers between devices: 4.4 us -> none  [passed_along(): return lax.ppermute(block, axis, route)]
  transfers between devices with their start and end apart: 8 -> 0, of which waited for: 8 -> 0; matrix products, arithmetic and copies ran while one was open for 9% -> 0% of each run, Pallas kernels for 0% -> 0%
where the time goes in v1:
time: 160 us
  Pallas kernels  150 us (94%)
  local copies, waits for them, and re-layouts  9.26 us (6%)
    pallas_call x1, Pallas kernels, fused_shards(): pl.pallas_call(functools.partial(relay_kernel, cap), name='relay', out_sh...  150 us
    unnamed x7, local copies, waits for them, and re-layouts  9.26 us

profile of v1, /device:TPU:28, one launch (start us, length us, event | category | flops | bytes accessed | tf_op | source)
XLA Modules:
  0.0 160.1 jit_solution(18271979022120563611)
XLA Ops:
  0.6 1.4 copy.11
  2.0 1.4 copy.12
  3.5 150.2 %relay.1 = (bf16[2,64,2048]{2,1,0:T(8,128)(2,1)}, bf16[384,2048]{1,0:T(8,128)(2,1)}, f32[384,2048]{1,0:T(8,128)}) custom-call(bf16[2,64,2048]{2,1,0:T(8,128)(2,1)} %bitcast.15, bf16[2,64,2048]{2,1,0:T(8,128)(2,1)} %og_ref.1, s32[2,64,2]{2,1,0:T(8,128)} %bitcast.18, f32[2,64,2]{2,1,0:T(8,128)} %bitcast.19, bf16[2048,384]{1,0:T(8,128)(2,1)} %bitcast.12, ...), custom_call_target="tpu_custom_call" | custom-call | tf_op jit(solution)/shard_map/relay/pallas_call | solution.py:487
  153.7 1.9 %copy.16 = bf16[1,2,64,2048]{3,2,1,0:T(8,128)(2,1)} copy(bf16[1,2,64,2048]{3,2,1,0:T(8,128)(2,1)} %bitcast.16) | data formatting | bytes 1048576
  155.5 0.0 copy-start
  155.5 2.9 %copy.17 = bf16[1,1,384,2048]{3,2,1,0:T(8,128)(2,1)} copy(bf16[1,1,384,2048]{3,2,1,0:T(8,128)(2,1)} %bitcast.11) | data formatting | bytes 3145728
  158.4 0.0 copy-done
  158.4 1.7 %copy.18 = f32[1,1,384,2048]{3,2,1,0:T(8,128)} copy(f32[1,1,384,2048]{3,2,1,0:T(8,128)S(1)} %bitcast.10) | data formatting | bytes 6291456
Async XLA Ops:
  155.5 2.9 %copy-start = (f32[384,2048]{1,0:T(8,128)S(1)}, f32[384,2048]{1,0:T(8,128)}, u32[]{:S(2)}) copy-start(f32[384,2048]{1,0:T(8,128)} %get-tuple-element.8) | copy-start | bytes 9437188

commit v2 on v1

--- a/solution.py
+++ b/solution.py
@@ -197,21 +197,32 @@
     dy_recv,
     dx_send,
     dx_recv,
+    x_peer,
+    g_peer,
+    part_send,
+    part_recv,
+    own_part,
     g_recv,
     gin,
     hid_g,
     hid_u,
     rot_t,
     rsq_t,
-    spread_x,
-    spread_dy,
+    spread_m,
     combine,
+    slot_w,
+    ids_peer,
+    rw_peer,
     rot_v,
     scale_v,
     w_sem,
     send_sem,
     recv_sem,
     self_sem,
+    swap_send,
+    swap_recv,
+    meta_send,
+    meta_recv,
     relay_send,
     relay_recv,
     out_sem,
@@ -223,10 +234,18 @@
     me = lax.axis_index("expert")
     seg = lax.axis_index("segment")
     micros, tokens, width = x_ref.shape
-    rows = n * cap
+    half = n // 2
+    local = lax.rem(me, half)
+    base = me - local
+    partner = lax.rem(me + half, n)
+    rows = half * cap
+    OWN, PEER = 0, 1
+    step = min(512, width)
+    pieces = [slice(c * step, (c + 1) * step) for c in range(width // step)]
     is_last = seg == segs - 1
-    is_first = seg == 0
+    inner = (me >= half) == (local < half // 2)
     X, DY, DX = 0, 1, 2
+    GX, GG, GP = 0, 1, 2
 
     weights = [
         pltpu.make_async_copy(src, dst, w_sem.at[i])
@@ -240,10 +259,12 @@
     barrier = pltpu.get_barrier_semaphore()
 
     def greet(d, carry):
-        pl.semaphore_signal(barrier, inc=1, device_id={"expert": lax.rem(me + d, n)})
+        peer = base + lax.rem(local + d, half)
+        pl.semaphore_signal(barrier, inc=1, device_id={"expert": peer})
         return carry
 
-    lax.fori_loop(1, n, greet, 0)
+    lax.fori_loop(1, half, greet, 0)
+    pl.semaphore_signal(barrier, inc=1, device_id={"expert": partner})
 
     @pl.when(seg > 0)
     def _():
@@ -253,106 +274,142 @@
     def _():
         pl.semaphore_signal(barrier, inc=1, device_id={"segment": seg + 1})
 
-    row_t = lax.broadcasted_iota(jnp.int32, (tokens, tokens), 0)
-    col_t = lax.broadcasted_iota(jnp.int32, (tokens, tokens), 1)
-    earlier = (row_t > col_t).astype(bf16)
-    lanes = lax.broadcasted_iota(jnp.int32, (tokens, n), 1)
-    slots_iota = lax.broadcasted_iota(jnp.int32, (tokens, rows), 1)
-    for m in range(micros):
-        ids0 = ids_ref[m, :, 0:1]
-        ids1 = ids_ref[m, :, 1:2]
-        hot0 = (lanes == ids0).astype(f32)
-        hot1 = (lanes == ids1).astype(f32)
-        prior = dot_f32(earlier, (hot0 + hot1).astype(bf16), ((1,), (0,)))
-        rank0 = jnp.sum(prior * hot0, axis=1, keepdims=True).astype(jnp.int32)
-        rank1 = jnp.sum(prior * hot1, axis=1, keepdims=True).astype(jnp.int32)
-        pick0 = (slots_iota == ids0 * cap + rank0).astype(f32)
-        pick1 = (slots_iota == ids1 * cap + rank1).astype(f32)
-        both = pick0 + pick1
-        combine[m] = both.astype(bf16)
-        spread_x[m] = jnp.transpose(both).astype(bf16)
-        spread_dy[m] = jnp.transpose(jnp.concatenate([pick0, pick1], axis=0)).astype(bf16)
-
-    def spread(m, matrix, values, dst):
-        step = min(512, width)
-        for c in range(width // step):
-            cols = slice(c * step, (c + 1) * step)
-            dst[m, :, cols] = dot_f32(matrix, values(cols), ((1,), (0,))).astype(bf16)
-
-    def block(i):
-        return pl.ds(pl.multiple_of(i * cap, cap), cap)
-
-    def push(kind, m, src, dst):
+    def block(side, i):
+        return pl.ds(pl.multiple_of(side * rows + i * cap, cap), cap)
+
+    def push(kind, side, m, src, dst):
+        here = block(side, local)
         pltpu.make_async_copy(
-            src.at[m, block(me)], dst.at[m, block(me)], self_sem.at[kind, m]
+            src.at[m, here], dst.at[m, here], self_sem.at[kind, side, m]
         ).start()
 
         def one(d, carry):
-            peer = lax.rem(me + d, n)
+            other = lax.rem(local + d, half)
             pltpu.make_async_remote_copy(
-                src_ref=src.at[m, block(peer)],
-                dst_ref=dst.at[m, block(me)],
-                send_sem=send_sem.at[kind, m],
-                recv_sem=recv_sem.at[kind, m],
-                device_id={"expert": peer},
+                src_ref=src.at[m, block(side, other)],
+                dst_ref=dst.at[m, here],
+                send_sem=send_sem.at[kind, side, m],
+                recv_sem=recv_sem.at[kind, side, m],
+                device_id={"expert": base + other},
             ).start()
             return carry
 
-        lax.fori_loop(1, n, one, 0)
-
-    def whole(kind, m, src, dst):
-        part = pl.ds(0, (n - 1) * cap)
+        lax.fori_loop(1, half, one, 0)
+
+    def whole(kind, side, m, src, dst):
+        part = pl.ds(side * rows, (half - 1) * cap)
         return pltpu.make_async_remote_copy(
             src_ref=src.at[m, part],
             dst_ref=dst.at[m, part],
-            send_sem=send_sem.at[kind, m],
-            recv_sem=recv_sem.at[kind, m],
-            device_id={"expert": lax.rem(me + 1, n)},
-        )
-
-    def arrive(kind, m, src, dst):
+            send_sem=send_sem.at[kind, side, m],
+            recv_sem=recv_sem.at[kind, side, m],
+            device_id={"expert": base + lax.rem(local + 1, half)},
+        )
+
+    def arrive(kind, side, m, src, dst):
+        here = block(side, local)
         pltpu.make_async_copy(
-            src.at[m, block(me)], dst.at[m, block(me)], self_sem.at[kind, m]
+            src.at[m, here], dst.at[m, here], self_sem.at[kind, side, m]
         ).wait()
-        whole(kind, m, src, dst).wait_recv()
-
-    def send_x(m):
-        spread(m, spread_x[m], lambda cols: x_ref[m, :, cols], x_send)
-        push(X, m, x_send, x_recv)
-
-    def send_dy(m, g_ref):
-        w0 = rw_ref[m, :, 0:1]
-        w1 = rw_ref[m, :, 1:2]
-
-        def values(cols):
-            g = g_ref[m, :, cols].astype(f32)
-            return jnp.concatenate([(w0 * g).astype(bf16), (w1 * g).astype(bf16)], axis=0)
-
-        spread(m, spread_dy[m], values, dy_send)
-        push(DY, m, dy_send, dy_recv)
+        whole(kind, side, m, src, dst).wait_recv()
+
+    def swap(kind, m, src, dst):
+        return pltpu.make_async_remote_copy(
+            src_ref=src.at[m],
+            dst_ref=dst.at[m],
+            send_sem=swap_send.at[kind, m],
+            recv_sem=swap_recv.at[kind, m],
+            device_id={"expert": partner},
+        )
+
+    metas = [
+        pltpu.make_async_remote_copy(
+            src_ref=src,
+            dst_ref=dst,
+            send_sem=meta_send.at[i],
+            recv_sem=meta_recv.at[i],
+            device_id={"expert": partner},
+        )
+        for i, (src, dst) in enumerate(((ids_ref, ids_peer), (rw_ref, rw_peer)))
+    ]
+
+    def matrices(side, ids, rw):
+        row_t = lax.broadcasted_iota(jnp.int32, (tokens, tokens), 0)
+        col_t = lax.broadcasted_iota(jnp.int32, (tokens, tokens), 1)
+        earlier = (row_t < col_t).astype(bf16)
+        experts = lax.broadcasted_iota(jnp.int32, (n, tokens), 0)
+        slots = lax.broadcasted_iota(jnp.int32, (rows, tokens), 0)
+        for m in range(micros):
+            ids0 = ids[m, 0:1, :]
+            ids1 = ids[m, 1:2, :]
+            hot0 = (experts == ids0).astype(f32)
+            hot1 = (experts == ids1).astype(f32)
+            prior = dot_f32((hot0 + hot1).astype(bf16), earlier, ((1,), (0,)))
+            rank0 = jnp.sum(prior * hot0, axis=0, keepdims=True).astype(jnp.int32)
+            rank1 = jnp.sum(prior * hot1, axis=0, keepdims=True).astype(jnp.int32)
+            pick0 = (slots == (ids0 - base) * cap + rank0).astype(f32)
+            pick1 = (slots == (ids1 - base) * cap + rank1).astype(f32)
+            both = pick0 + pick1
+            weighted = pick0 * rw[m, 0:1, :] + pick1 * rw[m, 1:2, :]
+            spread_m[m, side] = both.astype(bf16)
+            combine[m, side] = jnp.transpose(both).astype(bf16)
+            slot_w[m, side] = jnp.sum(weighted, axis=1, keepdims=True)
+
+    def send_x(side, m, src):
+        for cols in pieces:
+            moved = dot_f32(spread_m[m, side], src[m, :, cols], ((1,), (0,)))
+            x_send[m, side * rows : (side + 1) * rows, cols] = moved.astype(bf16)
+        push(X, side, m, x_send, x_recv)
+
+    def send_dy(side, m, src):
+        for cols in pieces:
+            moved = dot_f32(spread_m[m, side], src[m, :, cols], ((1,), (0,)))
+            dy_send[m, side * rows : (side + 1) * rows, cols] = (
+                slot_w[m, side] * moved
+            ).astype(bf16)
+        push(DY, side, m, dy_send, dy_recv)
+
+    def begin_x(m):
+        pl.when(inner)(swap(GX, m, x_ref, x_peer).start)
+        send_x(OWN, m, x_ref)
+        pl.when(jnp.logical_not(inner))(swap(GX, m, x_ref, x_peer).start)
+
+    def begin_dy(m, g_ref):
+        pl.when(inner)(swap(GG, m, g_ref, g_peer).start)
+        send_dy(OWN, m, g_ref)
+        pl.when(jnp.logical_not(inner))(swap(GG, m, g_ref, g_peer).start)
+
+    def peer_x(m):
+        swap(GX, m, x_ref, x_peer).wait_recv()
+        send_x(PEER, m, x_peer)
+
+    def peer_dy(m, g_ref):
+        swap(GG, m, g_ref, g_peer).wait_recv()
+        send_dy(PEER, m, g_peer)
 
     def forward(m):
-        arrive(X, m, x_send, x_recv)
+        arrive(X, OWN, m, x_send, x_recv)
+        arrive(X, PEER, m, x_send, x_recv)
         x = x_recv[m]
         hid_g[m] = dot_f32(x, gate[...], ((1,), (0,)))
         hid_u[m] = dot_f32(x, up[...], ((1,), (0,)))
 
     def backward(m):
-        arrive(DY, m, dy_send, dy_recv)
+        arrive(DY, OWN, m, dy_send, dy_recv)
+        arrive(DY, PEER, m, dy_send, dy_recv)
         grad_act = dot_f32(dy_recv[m], down[...], ((1,), (1,)))
         hg = hid_g[m]
         hu = hid_u[m]
         act, dact = silu_parts(hg)
         grad_gate = (grad_act * hu * dact).astype(bf16)
         grad_up = (grad_act * act).astype(bf16)
-        step = min(512, width)
-        for c in range(width // step):
-            cols = slice(c * step, (c + 1) * step)
+        for cols in pieces:
             dx_send[m, :, cols] = (
                 dot_f32(grad_gate, gate[cols, :], ((1,), (1,)))
                 + dot_f32(grad_up, up[cols, :], ((1,), (1,)))
             ).astype(bf16)
-        push(DX, m, dx_send, dx_recv)
+        push(DX, PEER, m, dx_send, dx_recv)
+        push(DX, OWN, m, dx_send, dx_recv)
 
     def rotate(m):
         act, _ = silu_parts(hid_g[m])
@@ -371,13 +428,22 @@
             device_id={"segment": lax.rem(seg + segs - 1, segs)},
         )
 
-    def gather_back(m, g_ref):
-        arrive(DX, m, dx_send, dx_recv)
-        step = min(512, width)
-        for c in range(width // step):
-            cols = slice(c * step, (c + 1) * step)
-            picked = dot_f32(combine[m], dx_recv[m, :, cols], ((1,), (0,)))
-            gin[m, :, cols] = (g_ref[m, :, cols].astype(f32) + picked).astype(bf16)
+    def half_back(m):
+        arrive(DX, PEER, m, dx_send, dx_recv)
+        for cols in pieces:
+            theirs = dot_f32(combine[m, PEER], dx_recv[m, rows:, cols], ((1,), (0,)))
+            part_send[m, :, cols] = theirs.astype(bf16)
+        swap(GP, m, part_send, part_recv).start()
+
+    def own_back(m, g_ref):
+        arrive(DX, OWN, m, dx_send, dx_recv)
+        for cols in pieces:
+            mine = dot_f32(combine[m, OWN], dx_recv[m, :rows, cols], ((1,), (0,)))
+            own_part[m, :, cols] = g_ref[m, :, cols].astype(f32) + mine
+
+    def finish(m):
+        swap(GP, m, part_send, part_recv).wait_recv()
+        gin[m] = (own_part[m] + part_recv[m].astype(f32)).astype(bf16)
 
         @pl.when(seg > 0)
         def _():
@@ -386,12 +452,12 @@
         pltpu.make_async_copy(gin.at[m], gin_out.at[m], out_sem.at[2 + m]).start()
 
     def statistics():
-        step = min(256, width)
+        part = min(256, width)
 
         def one(c, carry):
-            cols = pl.ds(pl.multiple_of(c * step, step), step)
-            grad = jnp.zeros((rot_v.shape[0], step), f32)
-            scale = jnp.zeros((rot_v.shape[0], step), f32)
+            cols = pl.ds(pl.multiple_of(c * part, part), part)
+            grad = jnp.zeros((rot_v.shape[0], part), f32)
+            scale = jnp.zeros((rot_v.shape[0], part), f32)
             for m in range(micros):
                 dy = dy_recv[m, :, cols]
                 wide = dy.astype(f32)
@@ -401,7 +467,7 @@
             scale_v[:, cols] = scale * (1.0 / micros)
             return carry
 
-        lax.fori_loop(0, width // step, one, 0)
+        lax.fori_loop(0, width // part, one, 0)
         pltpu.make_async_copy(rot_v, rot_out, out_sem.at[0]).start()
         pltpu.make_async_copy(scale_v, scale_out, out_sem.at[1]).start()
 
@@ -412,49 +478,101 @@
 
         lax.fori_loop(0, micros, one, 0)
 
+    matrices(OWN, ids_ref, rw_ref)
     neighbours = jnp.minimum(seg, 1) + jnp.minimum(segs - 1 - seg, 1)
-    pl.semaphore_wait(barrier, n - 1 + neighbours)
+    pl.semaphore_wait(barrier, half + neighbours)
+    for meta in metas:
+        meta.start()
 
     @pl.when(is_last)
     def _():
-        def first(m):
-            send_dy(m, og_ref)
-            send_x(m)
-
-        per_micro(first)
+        begin_dy(0, og_ref)
+        begin_x(0)
+        for meta in metas:
+            meta.wait_recv()
+        matrices(PEER, ids_peer, rw_peer)
         for w in weights:
             w.wait()
 
-        def second(m):
-            forward(m)
-            backward(m)
-
-        per_micro(second)
+        def through(m, carry):
+            peer_dy(m - 1, og_ref)
+            begin_dy(m, og_ref)
+            peer_x(m - 1)
+            begin_x(m)
+            forward(m - 1)
+            backward(m - 1)
+            return carry
+
+        lax.fori_loop(1, micros, through, 0)
+        peer_dy(micros - 1, og_ref)
+        peer_x(micros - 1)
+        forward(micros - 1)
+        backward(micros - 1)
+
+        def back(m):
+            half_back(m)
+            own_back(m, og_ref)
+            finish(m)
+
+        per_micro(back)
         per_micro(rotate)
-        per_micro(lambda m: gather_back(m, og_ref))
         statistics()
 
     @pl.when(jnp.logical_not(is_last))
     def _():
-        per_micro(send_x)
+        for meta in metas:
+            meta.wait_recv()
+        matrices(PEER, ids_peer, rw_peer)
+        begin_x(0)
+        peer_x(0)
         for w in weights:
             w.wait()
-        per_micro(forward)
-        per_micro(rotate)
-
-        def third(m):
+        forward(0)
+        rotate(0)
+
+        def begin(m):
             relay(m).wait_recv()
-            send_dy(m, g_recv)
-
-        per_micro(third)
-        per_micro(backward)
+            begin_dy(m, g_recv)
+
+        begin(0)
+
+        def through(m, carry):
+            begin_x(m)
+            peer_dy(m - 1, g_recv)
+            peer_x(m)
+            begin(m)
+            backward(m - 1)
+            forward(m)
+            rotate(m)
+            return carry
+
+        lax.fori_loop(1, micros, through, 0)
+        peer_dy(micros - 1, g_recv)
+        backward(micros - 1)
+        half_back(0)
         statistics()
-        per_micro(lambda m: gather_back(m, g_recv))
+        own_back(0, g_recv)
+        finish(0)
+
+        def back(m, carry):
+            half_back(m)
+            own_back(m, g_recv)
+            finish(m)
+            return carry
+
+        lax.fori_loop(1, micros, back, 0)
+
+    for meta in metas:
+        meta.wait_send()
 
     def drain(m):
-        whole(X, m, x_send, x_recv).wait_send()
-        whole(DY, m, dy_send, dy_recv).wait_send()
-        whole(DX, m, dx_send, dx_recv).wait_send()
+        for side in (OWN, PEER):
+            whole(X, side, m, x_send, x_recv).wait_send()
+            whole(DY, side, m, dy_send, dy_recv).wait_send()
+            whole(DX, side, m, dx_send, dx_recv).wait_send()
+        swap(GX, m, x_ref, x_peer).wait_send()
+        swap(GG, m, g_recv, g_peer).wait_send()
+        swap(GP, m, part_send, part_recv).wait_send()
 
         @pl.when(seg > 0)
         def _():
@@ -473,7 +591,7 @@
     n = lax.axis_size("expert")
     micros, tokens, width = saved_input.shape[1:]
     cap = max(2, 4 * tokens // n)
-    if cap % 16:
+    if cap % 16 or n % 2:
         return shards(
             saved_input, out_grad, expert_ids, router_weights, w_gate, w_up, w_down, eigenbasis
         )
@@ -483,7 +601,9 @@
     f32 = jnp.float32
     vmem = pl.BlockSpec(memory_space=pltpu.VMEM)
     anywhere = pl.BlockSpec(memory_space=pl.ANY)
+    in_hbm = pl.BlockSpec(memory_space=pltpu.MemorySpace.HBM)
     routed = pltpu.VMEM((micros, rows, width), bf16)
+    block = pltpu.VMEM((micros, tokens, width), bf16)
     grad_in, rotated_grad, scales = pl.pallas_call(
         functools.partial(relay_kernel, cap),
         name="relay",
@@ -492,7 +612,7 @@
             jax.ShapeDtypeStruct((hidden, width), bf16),
             jax.ShapeDtypeStruct((hidden, width), f32),
         ),
-        in_specs=[vmem] * 4 + [anywhere] * 4,
+        in_specs=[vmem] * 4 + [in_hbm] * 4,
         out_specs=(anywhere, anywhere, anywhere),
         scratch_shapes=[
             pltpu.VMEM((width, hidden), bf16),
@@ -505,21 +625,32 @@
             routed,
             routed,
             routed,
-            pltpu.VMEM((micros, tokens, width), bf16),
-            pltpu.VMEM((micros, tokens, width), bf16),
+            block,
+            block,
+            block,
+            block,
+            pltpu.VMEM((micros, tokens, width), f32),
+            block,
+            block,
             pltpu.VMEM((micros, rows, hidden), f32),
             pltpu.VMEM((micros, rows, hidden), f32),
             pltpu.VMEM((micros, hidden, rows), bf16),
             pltpu.VMEM((micros, hidden, rows), bf16),
-            pltpu.VMEM((micros, rows, tokens), bf16),
-            pltpu.VMEM((micros, rows, 2 * tokens), bf16),
-            pltpu.VMEM((micros, tokens, rows), bf16),
+            pltpu.VMEM((micros, 2, rows // 2, tokens), bf16),
+            pltpu.VMEM((micros, 2, tokens, rows // 2), bf16),
+            pltpu.VMEM((micros, 2, rows // 2, 1), f32),
+            pltpu.VMEM((micros, 2, tokens), jnp.int32),
+            pltpu.VMEM((micros, 2, tokens), f32),
             pltpu.VMEM((hidden, width), bf16),
             pltpu.VMEM((hidden, width), f32),
             pltpu.SemaphoreType.DMA((4,)),
+            pltpu.SemaphoreType.DMA((3, 2, micros)),
+            pltpu.SemaphoreType.DMA((3, 2, micros)),
+            pltpu.SemaphoreType.DMA((3, 2, micros)),
             pltpu.SemaphoreType.DMA((3, micros)),
             pltpu.SemaphoreType.DMA((3, micros)),
-            pltpu.SemaphoreType.DMA((3, micros)),
+            pltpu.SemaphoreType.DMA((2,)),
+            pltpu.SemaphoreType.DMA((2,)),
             pltpu.SemaphoreType.DMA((micros,)),
             pltpu.SemaphoreType.DMA((micros,)),
             pltpu.SemaphoreType.DMA((2 + micros,)),
@@ -530,8 +661,8 @@
     )(
         saved_input[0],
         out_grad,
-        expert_ids[0],
-        router_weights[0],
+        jnp.swapaxes(expert_ids[0], 1, 2),
+        jnp.swapaxes(router_weights[0], 1, 2),
         w_gate[0, 0],
         w_up[0, 0],
         w_down[0, 0],

time: 160 us -> 138 us (0.86); the launches traced: 160 us -> 136 us
  Pallas kernels: 150 us -> 129 us
  local copies, waits for them, and re-layouts: 9.26 us -> 6.43 us
    pallas_call x1, Pallas kernels: 150 us -> 129 us  [fused_shards(): pl.pallas_call(functools.partial(relay_kernel, cap), name='relay', out_sh...]
    unnamed x7 -> x5, local copies, waits for them, and re-layouts: 9.26 us -> 6.43 us
where the time goes in v2:
time: 138 us; the launch traced here: 136 us
  Pallas kernels  129 us (93%)
  local copies, waits for them, and re-layouts  6.43 us (5%)
    pallas_call x1, Pallas kernels, fused_shards(): pl.pallas_call(functools.partial(relay_kernel, cap), name='relay', out_sh...  129 us
    unnamed x5, local copies, waits for them, and re-layouts  6.43 us

profile of v2, /device:TPU:28, one launch (start us, length us, event | category | flops | bytes accessed | tf_op | source)
XLA Modules:
  0.0 136.1 jit_solution(17778768679973736681)
XLA Ops:
  0.6 129.1 %relay.1 = (bf16[2,64,2048]{2,1,0:T(8,128)(2,1)}, bf16[384,2048]{1,0:T(8,128)(2,1)}, f32[384,2048]{1,0:T(8,128)}) custom-call(bf16[2,64,2048]{2,1,0:T(8,128)(2,1)} %bitcast.20, bf16[2,64,2048]{2,1,0:T(8,128)(2,1)} %og_ref.1, s32[2,2,64]{2,1,0:T(2,128)} %bitcast.22, f32[2,2,64]{2,1,0:T(2,128)} %bitcast.23, bf16[2048,384]{1,0:T(8,128)(2,1)} %bitcast.16, ...), custom_call_target="tpu_custom_call" | custom-call | tf_op jit(solution)/shard_map/relay/pallas_call | solution.py:607
  129.7 1.9 %copy.14 = bf16[1,2,64,2048]{3,2,1,0:T(8,128)(2,1)} copy(bf16[1,2,64,2048]{3,2,1,0:T(8,128)(2,1)} %bitcast.19) | data formatting | bytes 1048576
  131.6 0.0 copy-start
  131.6 2.9 %copy.15 = bf16[1,1,384,2048]{3,2,1,0:T(8,128)(2,1)} copy(bf16[1,1,384,2048]{3,2,1,0:T(8,128)(2,1)} %bitcast.15) | data formatting | bytes 3145728
  134.5 0.0 copy-done
  134.5 1.7 %copy.16 = f32[1,1,384,2048]{3,2,1,0:T(8,128)} copy(f32[1,1,384,2048]{3,2,1,0:T(8,128)S(1)} %bitcast.14) | data formatting | bytes 6291456
Async XLA Ops:
  131.6 2.9 %copy-start = (f32[384,2048]{1,0:T(8,128)S(1)}, f32[384,2048]{1,0:T(8,128)}, u32[]{:S(2)}) copy-start(f32[384,2048]{1,0:T(8,128)} %get-tuple-element.8) | copy-start | bytes 9437188

commit v3 on v2

--- a/solution.py
+++ b/solution.py
@@ -226,6 +226,7 @@
     relay_send,
     relay_recv,
     out_sem,
+    go_sem,
 ):
     bf16 = jnp.bfloat16
     f32 = jnp.float32
@@ -505,6 +506,8 @@
 
         lax.fori_loop(1, micros, through, 0)
         peer_dy(micros - 1, og_ref)
+        if segs > 1:
+            pl.semaphore_signal(go_sem, inc=1, device_id={"segment": seg - 1})
         peer_x(micros - 1)
         forward(micros - 1)
         backward(micros - 1)
@@ -523,6 +526,11 @@
         for meta in metas:
             meta.wait_recv()
         matrices(PEER, ids_peer, rw_peer)
+
+        @pl.when(seg == segs - 2)
+        def _():
+            pl.semaphore_wait(go_sem, 1)
+
         begin_x(0)
         peer_x(0)
         for w in weights:
@@ -654,6 +662,7 @@
             pltpu.SemaphoreType.DMA((micros,)),
             pltpu.SemaphoreType.DMA((micros,)),
             pltpu.SemaphoreType.DMA((2 + micros,)),
+            pltpu.SemaphoreType.REGULAR,
         ],
         compiler_params=pltpu.CompilerParams(
             collective_id=0, has_side_effects=True, vmem_limit_bytes=62 << 20

time: 138 us -> 134 us (0.971)
  Pallas kernels: 129 us -> 125 us
    pallas_call x1, Pallas kernels: 129 us -> 125 us  [fused_shards(): pl.pallas_call(functools.partial(relay_kernel, cap), name='relay', out_sh...]
where the time goes in v3:
time: 134 us; the launch traced here: 132 us
  Pallas kernels  125 us (93%)
  local copies, waits for them, and re-layouts  6.43 us (5%)
    pallas_call x1, Pallas kernels, fused_shards(): pl.pallas_call(functools.partial(relay_kernel, cap), name='relay', out_sh...  125 us
    unnamed x5, local copies, waits for them, and re-layouts  6.43 us

profile of v3, /device:TPU:28, one launch (start us, length us, event | category | flops | bytes accessed | tf_op | source)
XLA Modules:
  0.0 132.0 jit_solution(14597430685858293999)
XLA Ops:
  0.6 125.0 %relay.1 = (bf16[2,64,2048]{2,1,0:T(8,128)(2,1)}, bf16[384,2048]{1,0:T(8,128)(2,1)}, f32[384,2048]{1,0:T(8,128)}) custom-call(bf16[2,64,2048]{2,1,0:T(8,128)(2,1)} %bitcast.20, bf16[2,64,2048]{2,1,0:T(8,128)(2,1)} %og_ref.1, s32[2,2,64]{2,1,0:T(2,128)} %bitcast.22, f32[2,2,64]{2,1,0:T(2,128)} %bitcast.23, bf16[2048,384]{1,0:T(8,128)(2,1)} %bitcast.16, ...), custom_call_target="tpu_custom_call" | custom-call | tf_op jit(solution)/shard_map/relay/pallas_call | solution.py:615
  125.6 1.9 %copy.14 = bf16[1,2,64,2048]{3,2,1,0:T(8,128)(2,1)} copy(bf16[1,2,64,2048]{3,2,1,0:T(8,128)(2,1)} %bitcast.19) | data formatting | bytes 1048576
  127.5 0.0 copy-start
  127.5 2.9 %copy.15 = bf16[1,1,384,2048]{3,2,1,0:T(8,128)(2,1)} copy(bf16[1,1,384,2048]{3,2,1,0:T(8,128)(2,1)} %bitcast.15) | data formatting | bytes 3145728
  130.4 0.0 copy-done
  130.4 1.7 %copy.16 = f32[1,1,384,2048]{3,2,1,0:T(8,128)} copy(f32[1,1,384,2048]{3,2,1,0:T(8,128)S(1)} %bitcast.14) | data formatting | bytes 6291456
Async XLA Ops:
  127.5 2.9 %copy-start = (f32[384,2048]{1,0:T(8,128)S(1)}, f32[384,2048]{1,0:T(8,128)}, u32[]{:S(2)}) copy-start(f32[384,2048]{1,0:T(8,128)} %get-tuple-element.8) | copy-start | bytes 9437188
